TPU v7x, 32 devices: a whole 2x2x4 slice. The times are simulated.
32 devices in a mesh: shard: 4 (over x, core), seq: 8 (over z, y).
Axes of the slice: x: 2, y: 2, z: 4, core: 2. Of those that a mesh axis runs over, the one named last changes fastest.
Arguments:
- hidden: bfloat16 [16384, 1536], P(('shard', 'seq')), may hold values from -6 to 6
- cotangent: bfloat16 [16384, 1536], P(('shard', 'seq')), may hold values from -6 to 6
- seg_ids: int32 [16384], replicated, may hold values from 0 to 7, never falling along the last dimension, each value on 1 to 4096 neighbouring positions
- norm_gain: bfloat16 [1536], P('shard'), may hold values from 0.5 to 1.5
- in_weight: bfloat16 [1536, 6448], P('shard'), may hold values from -0.15625 to 0.15625
- conv_weight: bfloat16 [4, 3328], P(None, 'shard'), may hold values from -3 to 3
- conv_bias: bfloat16 [3328], P('shard'), may hold values from -3 to 3
- dt_bias: bfloat16 [48], replicated, may hold values from -8 to -2
- a_log: bfloat16 [48], replicated, may hold values from 0 to 2.6875
- d_skip: bfloat16 [48], replicated, may hold values from 0.5 to 1.5
- out_gain: bfloat16 [3072], P('shard'), may hold values from 0.5 to 1.5
- out_weight: bfloat16 [3072, 1536], P('shard'), may hold values from -0.109375 to 0.109375
Outputs:
- block_out: bfloat16 [16384, 1536], P(('shard', 'seq'))
- grad_hidden: float32 [16384, 1536], P(('shard', 'seq'))
- grad_norm_gain: float32 [1536], P(('shard', 'seq'))
- grad_in_weight: float32 [1536, 6448], P(('shard', 'seq'))
- grad_conv_weight: float32 [4, 3328], P(None, ('shard', 'seq'))
- grad_conv_bias: float32 [3328], P(('shard', 'seq'))
- grad_dt_bias: float32 [48], replicated
- grad_a_log: float32 [48], replicated
- grad_d_skip: float32 [48], replicated
- grad_out_gain: float32 [3072], P(('shard', 'seq'))
- grad_out_weight: float32 [3072, 1536], P(('shard', 'seq'))
Inputs may be any that keep to these rules, and one draw needn't show every extreme that they name: seg_ids never falls along the tokens; every value occurs; each document holds 1 to 4096 tokens and one holds exactly 4096.
All inputs are finite; a program needn't handle non-finite values.
Results may differ from a plain program's by a relative error of at most 0.02.
Values may be sent and summed in bfloat16 or wider, within the bound.
No kernel may reach another device: no remote copies, remote signals or barrier semaphores. Data moves between devices by JAX's collectives and lax.ppermute only.
A program may use at most 384 MiB of HBM per device.

v0:
```python
import jax
import jax.numpy as jnp
from jax import lax
from jax.sharding import PartitionSpec as P

HEAD_DIM = 64
CONV = 4
BLOCK = 256
HIGH = lax.Precision.HIGHEST
EPS = 1e-05


def from_behind(value, axis, steps):
    count = lax.axis_size(axis)
    initial, last = (max(0, -steps), min(count, count - steps))
    return lax.ppermute(value, axis, [(source, source + steps) for source in range(initial, last)])


def prefix(array, axis, join, neutral, backward):
    count = lax.axis_size(axis)
    place = lax.axis_index(axis)
    ahead = count - 1 - place if backward else place
    gathered = jax.tree.map(
        lambda a, kind: lax.all_gather(a.astype(kind), axis), array, (jnp.bfloat16, jnp.bfloat16)
    )
    state = jax.tree.map(lambda a, e: jnp.zeros_like(a) + jnp.asarray(e, a.dtype), array, neutral)

    def one(step, state):
        source = count - 1 - step if backward else step
        return join(
            state,
            jax.tree.map(
                lambda a, own: lax.dynamic_index_in_dim(a, source, 0, False).astype(own.dtype),
                gathered,
                array,
            ),
        )

    return lax.fori_loop(0, ahead, one, state)


def token_norm(values, gain):
    scale = lax.rsqrt(jnp.mean(values * values, axis=1, keepdims=True) + EPS)
    return values * scale * gain[None, :]


def gate_norm(mixer_out, gate_z, gain):
    gated = mixer_out * jax.nn.silu(gate_z)
    scale = lax.rsqrt(jnp.mean(gated * gated, axis=1, keepdims=True) + EPS)
    return gated * scale * gain[None, :]


def chain_pairs(earlier, later):
    return (earlier[0] * later[0], later[0][None, :] * earlier[1] + later[1])


def causal_conv(extended, seg_ext, weight, bias, length):
    seg_here = seg_ext[CONV - 1 :]
    summed = jnp.zeros((length, extended.shape[1]), jnp.float32) + bias[None, :]
    for tap in range(CONV):
        same_doc = (seg_ext[tap : tap + length] == seg_here).astype(jnp.float32)
        summed = summed + weight[tap][None, :] * extended[tap : tap + length] * same_doc[:, None]
    return jax.nn.silu(summed)


def make_mixer(seg_ext, head_lo, channel_lo):

    def mixer(
        x_raw,
        bc_raw,
        dt_raw,
        tail_x,
        tail_bc,
        conv_x,
        bias_x,
        conv_bc,
        bias_bc,
        dt_bias,
        a_log,
        d_skip,
    ):
        length = x_raw.shape[0]
        chan_width = x_raw.shape[1]
        n_state = bc_raw.shape[1] // 2
        local_heads = (chan_width - 1) // HEAD_DIM + 2
        seg_here = seg_ext[CONV - 1 :]
        x_conv = causal_conv(jnp.concatenate([tail_x, x_raw], 0), seg_ext, conv_x, bias_x, length)
        bc_conv = causal_conv(
            jnp.concatenate([tail_bc, bc_raw], 0), seg_ext, conv_bc, bias_bc, length
        )
        b_mat = bc_conv[:, :n_state]
        c_mat = bc_conv[:, n_state:]
        step_size = jax.nn.softplus(dt_raw + dt_bias[None, :])
        log_decay = -step_size * jnp.exp(a_log)[None, :]
        padding = jnp.zeros((length, local_heads - 1), jnp.float32)
        step_local = lax.dynamic_slice_in_dim(
            jnp.concatenate([step_size, padding], 1), head_lo, local_heads, 1
        )
        decay_local = lax.dynamic_slice_in_dim(
            jnp.concatenate([log_decay, padding], 1), head_lo, local_heads, 1
        )
        skip_local = lax.dynamic_slice_in_dim(
            jnp.concatenate([d_skip, jnp.zeros((local_heads - 1,), jnp.float32)]),
            head_lo,
            local_heads,
        )
        owner = (channel_lo + jnp.arange(chan_width, dtype=jnp.int32)) // HEAD_DIM - head_lo
        select = (owner[None, :] == jnp.arange(local_heads, dtype=jnp.int32)[:, None]).astype(
            jnp.float32
        )
        x_step = x_conv * jnp.dot(step_local, select, precision=HIGH)
        n_blocks = length // BLOCK
        seg_before = seg_ext[CONV - 2 : CONV - 2 + length].reshape(n_blocks, BLOCK)[:, 0]

        def block_step(state, inputs):
            x_block, b_block, c_block, decay_block, seg_block, seg_prior = inputs
            cum_decay = jnp.cumsum(decay_block, axis=0)
            positions = jnp.arange(BLOCK, dtype=jnp.int32)
            same_doc = (seg_block[:, None] == seg_block[None, :]) & (
                positions[:, None] >= positions[None, :]
            )
            log_gap = cum_decay.T[:, :, None] - cum_decay.T[:, None, :]
            weights = jnp.exp(jnp.where(same_doc[None], log_gap, -jnp.inf))
            scores = jnp.dot(c_block, b_block.T, precision=HIGH)
            per_head = jnp.einsum("jts,sc->jtc", weights * scores[None], x_block, precision=HIGH)
            inside = jnp.sum(per_head * select[:, None, :], axis=0)
            entering = jnp.exp(cum_decay) * (seg_block == seg_prior).astype(jnp.float32)[:, None]
            enter_block = jnp.dot(entering, select, precision=HIGH)
            from_state = jnp.dot(c_block, state, precision=HIGH) * enter_block
            keep_tail = jnp.exp(
                jnp.where(
                    (seg_block == seg_block[BLOCK - 1])[:, None],
                    cum_decay[BLOCK - 1][None, :] - cum_decay,
                    -jnp.inf,
                )
            )
            tail_channels = jnp.dot(keep_tail, select, precision=HIGH)
            new_state = enter_block[BLOCK - 1][None, :] * state + jnp.dot(
                b_block.T, x_block * tail_channels, precision=HIGH
            )
            return (new_state, inside + from_state)

        inputs = (
            x_step.reshape(n_blocks, BLOCK, chan_width),
            b_mat.reshape(n_blocks, BLOCK, n_state),
            c_mat.reshape(n_blocks, BLOCK, n_state),
            decay_local.reshape(n_blocks, BLOCK, local_heads),
            seg_here.reshape(n_blocks, BLOCK),
            seg_before,
        )
        final_state, block_out = lax.scan(
            jax.checkpoint(block_step), jnp.zeros((n_state, chan_width), jnp.float32), inputs
        )
        skip_channels = jnp.dot(skip_local, select, precision=HIGH)
        mixer_out = block_out.reshape(length, chan_width) + x_conv * skip_channels[None, :]
        part_cum = jnp.cumsum(decay_local, axis=0)
        carried_in = (seg_here == seg_ext[CONV - 2]).astype(jnp.float32)
        enter = jnp.dot(jnp.exp(part_cum) * carried_in[:, None], select, precision=HIGH)
        return (mixer_out, final_state, enter, c_mat)

    return mixer


def on_device(
    hidden,
    cotangent,
    seg_ids,
    norm_gain,
    in_weight,
    conv_weight,
    conv_bias,
    dt_bias,
    a_log,
    d_skip,
    out_gain,
    out_weight,
):
    gains_in, w_in, w_conv, b_conv, gains_out, w_out = (
        lax.all_gather(norm_gain, "shard", axis=0, tiled=True),
        lax.all_gather(in_weight, "shard", axis=0, tiled=True),
        lax.all_gather(conv_weight, "shard", axis=1, tiled=True),
        lax.all_gather(conv_bias, "shard", axis=0, tiled=True),
        lax.all_gather(out_gain, "shard", axis=0, tiled=True),
        lax.all_gather(out_weight, "shard", axis=0, tiled=True),
    )
    seq_count = lax.axis_size("seq")
    shard_count = lax.axis_size("shard")
    seq_rank = lax.axis_index("seq")
    shard_rank = lax.axis_index("shard")
    tok_len = hidden.shape[0]
    inner_width = w_out.shape[0]
    n_state = (w_conv.shape[1] - inner_width) // 2
    chan_width = inner_width // seq_count
    part_len = tok_len * seq_count
    hidden_f = hidden.astype(jnp.float32)
    gains_f = gains_in.astype(jnp.float32)
    normed_in = token_norm(hidden_f, gains_f).astype(jnp.bfloat16)
    projected = jnp.dot(normed_in, w_in, preferred_element_type=jnp.float32).astype(jnp.bfloat16)
    gate_z = projected[:, :inner_width]
    x_tokens = projected[:, inner_width : 2 * inner_width]
    shared_tokens = projected[:, 2 * inner_width :]
    x_heads = lax.all_to_all(x_tokens, "seq", split_axis=1, concat_axis=0, tiled=True)
    shared = lax.all_gather(shared_tokens, "seq", axis=0, tiled=True)
    bc_heads = shared[:, : 2 * n_state]
    tail_x, tail_bc = from_behind(
        (x_heads[part_len - CONV + 1 :], bc_heads[part_len - CONV + 1 :]), "shard", 1
    )
    lead = jnp.full((CONV - 1,), -1, jnp.int32)
    seg_all = jnp.concatenate([lead, seg_ids])
    seg_ext = lax.dynamic_slice_in_dim(seg_all, shard_rank * part_len, part_len + CONV - 1)
    channel_lo = seq_rank * chan_width
    head_lo = channel_lo // HEAD_DIM
    conv_f = w_conv.astype(jnp.float32)
    bias_f = b_conv.astype(jnp.float32)
    primals = (
        x_heads.astype(jnp.float32),
        bc_heads.astype(jnp.float32),
        shared[:, 2 * n_state :].astype(jnp.float32),
        tail_x.astype(jnp.float32),
        tail_bc.astype(jnp.float32),
        lax.dynamic_slice_in_dim(conv_f, channel_lo, chan_width, 1),
        lax.dynamic_slice_in_dim(bias_f, channel_lo, chan_width, 0),
        conv_f[:, inner_width:],
        bias_f[inner_width:],
        dt_bias.astype(jnp.float32),
        a_log.astype(jnp.float32),
        d_skip.astype(jnp.float32),
    )
    mixer = make_mixer(seg_ext, head_lo, channel_lo)
    mixer_outs, mixer_pull = jax.vjp(mixer, *primals)
    local_out, state_local, enter, c_mat = mixer_outs
    identity = (jnp.ones((chan_width,), jnp.float32), jnp.zeros((n_state, chan_width), jnp.float32))
    state_in = prefix((enter[part_len - 1], state_local), "shard", chain_pairs, identity, False)[1]
    carried = jnp.dot(c_mat, state_in, precision=HIGH)
    mixer_full = local_out + carried * enter
    mixer_tokens = lax.all_to_all(
        mixer_full.astype(jnp.bfloat16), "seq", split_axis=0, concat_axis=1, tiled=True
    )
    normed_f, gate_pull = jax.vjp(
        gate_norm,
        mixer_tokens.astype(jnp.float32),
        gate_z.astype(jnp.float32),
        gains_out.astype(jnp.float32),
    )
    normed_out = normed_f.astype(jnp.bfloat16)
    branch = jnp.dot(normed_out, w_out, preferred_element_type=jnp.float32)
    block_out = (hidden_f + branch).astype(jnp.bfloat16)
    grad_out_w = lax.dot_general(
        normed_out, cotangent, (((0,), (0,)), ((), ())), preferred_element_type=jnp.float32
    )
    d_normed = lax.dot_general(
        cotangent, w_out, (((1,), (1,)), ((), ())), preferred_element_type=jnp.float32
    )
    d_mixer, d_gate_z, d_gain_out = gate_pull(d_normed)
    d_heads = lax.all_to_all(
        d_mixer.astype(jnp.bfloat16), "seq", split_axis=1, concat_axis=0, tiled=True
    ).astype(jnp.float32)
    weighted = d_heads * enter
    d_state_local = jnp.dot(c_mat.T, weighted, precision=HIGH)
    d_state_out = prefix(
        (enter[part_len - 1], d_state_local), "shard", chain_pairs, identity, True
    )[1]
    d_enter = d_heads * carried
    d_enter = d_enter.at[part_len - 1].add(jnp.sum(d_state_out * state_in, axis=0))
    d_c_mat = jnp.dot(weighted, state_in.T, precision=HIGH)
    mixer_grads = mixer_pull((d_heads, d_state_out, d_enter, d_c_mat))
    (
        d_x_raw,
        d_bc_raw,
        d_dt_raw,
        d_tail_x,
        d_tail_bc,
        d_conv_x,
        d_bias_x,
        d_conv_bc,
        d_bias_bc,
        d_dt_bias,
        d_a_log,
        d_d_skip,
    ) = mixer_grads
    back_x, back_bc = from_behind((d_tail_x, d_tail_bc), "shard", -1)
    d_x_raw = d_x_raw.at[part_len - CONV + 1 :].add(back_x)
    d_bc_raw = d_bc_raw.at[part_len - CONV + 1 :].add(back_bc)
    d_x_tokens = lax.all_to_all(
        d_x_raw.astype(jnp.bfloat16), "seq", split_axis=0, concat_axis=1, tiled=True
    )
    d_shared = lax.psum_scatter(
        jnp.concatenate([d_bc_raw, d_dt_raw], 1).astype(jnp.bfloat16),
        "seq",
        scatter_dimension=0,
        tiled=True,
    ).astype(jnp.float32)
    d_projected = jnp.concatenate([d_gate_z, d_x_tokens.astype(jnp.float32), d_shared], 1).astype(
        jnp.bfloat16
    )
    grad_in_w = lax.dot_general(
        normed_in, d_projected, (((0,), (0,)), ((), ())), preferred_element_type=jnp.float32
    )
    d_normed_in = lax.dot_general(
        d_projected, w_in, (((1,), (1,)), ((), ())), preferred_element_type=jnp.float32
    )
    _, norm_pull = jax.vjp(token_norm, hidden_f, gains_f)
    d_hidden_norm, d_gain_in = norm_pull(d_normed_in)
    grad_hidden = cotangent.astype(jnp.float32) + d_hidden_norm
    conv_grad = jnp.zeros(w_conv.shape, jnp.float32)
    conv_grad = lax.dynamic_update_slice(conv_grad, d_conv_x, (jnp.int32(0), channel_lo))
    conv_grad = conv_grad.at[:, inner_width:].set(d_conv_bc)
    bias_grad = jnp.zeros(b_conv.shape, jnp.float32)
    bias_grad = lax.dynamic_update_slice(bias_grad, d_bias_x, (channel_lo,))
    bias_grad = bias_grad.at[inner_width:].set(d_bias_bc)
    head_grads = jnp.concatenate([d_dt_bias, d_a_log, d_d_skip])
    n_heads = dt_bias.shape[0]
    head_rows = jnp.broadcast_to(
        head_grads[None, :], (shard_count * seq_count, head_grads.shape[0])
    )
    partial_sums = (
        lax.psum_scatter(
            d_gain_in.astype(jnp.bfloat16), "shard", scatter_dimension=0, tiled=True
        ).astype(jnp.float32),
        lax.psum_scatter(
            grad_in_w.astype(jnp.bfloat16), "shard", scatter_dimension=0, tiled=True
        ).astype(jnp.float32),
        lax.psum_scatter(
            conv_grad.astype(jnp.bfloat16), "shard", scatter_dimension=1, tiled=True
        ).astype(jnp.float32),
        lax.psum_scatter(
            bias_grad.astype(jnp.bfloat16), "shard", scatter_dimension=0, tiled=True
        ).astype(jnp.float32),
        lax.psum_scatter(
            d_gain_out.astype(jnp.bfloat16), "shard", scatter_dimension=0, tiled=True
        ).astype(jnp.float32),
        lax.psum_scatter(
            grad_out_w.astype(jnp.bfloat16), "shard", scatter_dimension=0, tiled=True
        ).astype(jnp.float32),
        lax.psum_scatter(
            head_rows.astype(jnp.bfloat16), "shard", scatter_dimension=0, tiled=True
        ).astype(jnp.float32),
    )
    reduced = (
        lax.psum_scatter(
            partial_sums[0].astype(jnp.bfloat16), "seq", scatter_dimension=0, tiled=True
        ).astype(jnp.float32),
        lax.psum_scatter(
            partial_sums[1].astype(jnp.bfloat16), "seq", scatter_dimension=0, tiled=True
        ).astype(jnp.float32),
        lax.psum_scatter(
            partial_sums[2].astype(jnp.bfloat16), "seq", scatter_dimension=1, tiled=True
        ).astype(jnp.float32),
        lax.psum_scatter(
            partial_sums[3].astype(jnp.bfloat16), "seq", scatter_dimension=0, tiled=True
        ).astype(jnp.float32),
        lax.psum_scatter(
            partial_sums[4].astype(jnp.bfloat16), "seq", scatter_dimension=0, tiled=True
        ).astype(jnp.float32),
        lax.psum_scatter(
            partial_sums[5].astype(jnp.bfloat16), "seq", scatter_dimension=0, tiled=True
        ).astype(jnp.float32),
        lax.psum_scatter(
            partial_sums[6].astype(jnp.bfloat16), "seq", scatter_dimension=0, tiled=True
        ).astype(jnp.float32),
    )
    head_total = reduced[6][0]
    return (
        block_out,
        grad_hidden,
        reduced[0],
        reduced[1],
        reduced[2],
        reduced[3],
        head_total[:n_heads],
        head_total[n_heads : 2 * n_heads],
        head_total[2 * n_heads :],
        reduced[4],
        reduced[5],
    )


def solution(mesh):
    return jax.shard_map(
        on_device,
        mesh=mesh,
        in_specs=(
            P(("shard", "seq"), None),
            P(("shard", "seq"), None),
            P(),
            P("shard"),
            P("shard", None),
            P(None, "shard"),
            P("shard"),
            P(),
            P(),
            P(),
            P("shard"),
            P("shard", None),
        ),
        out_specs=(
            P(("shard", "seq"), None),
            P(("shard", "seq"), None),
            P(("shard", "seq")),
            P(("shard", "seq"), None),
            P(None, ("shard", "seq")),
            P(("shard", "seq")),
            P(),
            P(),
            P(),
            P(("shard", "seq")),
            P(("shard", "seq"), None),
        ),
        check_vma=False,
    )
```

profile of v0, /device:TPU:0, one launch (start us, length us, event | category | flops | bytes accessed | tf_op | source)
XLA Modules:
  0.0 2106.3 jit_solution(14078692126944660812)
XLA Ops:
  15.2 122.0 %all-gather.10.cloned.1.call-done = bf16[1536,6448]{0,1:T(8,128)(2,1)} async-done(((bf16[384,6448]{0,1:T(8,128)(2,1)}), bf16[1536,6448]{0,1:T(8,128)(2,1)}) %all-gather.10.cloned.1.call-update) | async-done | bytes 19808272 | tf_op jit(solution)/shard_map/all_gather | solution.py:180
  137.2 15.2 convolution_convert_fusion.2
  185.2 47.3 %all-gather.12.cloned.1.call-done = bf16[4096,304]{0,1:T(8,128)(2,1)} async-done(((bf16[512,304]{0,1:T(8,128)(2,1)}), bf16[4096,304]{0,1:T(8,128)(2,1)}) %all-gather.12.cloned.1.call-update) | async-done | bytes 2490384 | tf_op jit(solution)/shard_map/all_gather | solution.py:203
  286.1 19.9 fusion.198
  309.5 309.7 %while.75 = (s32[]{:T(128)}, f32[128,384]{1,0:T(8,128)S(1)}, f32[16,256,384]{2,1,0:T(8,128)}, f32[16,128,384]{2,1,0:T(8,128)}, f32[16,256,7]{1,2,0:T(8,128)}, /*...) while((s32[]{:T(128)}, f32[128,384]{1,0:T(8,128)S(1)}, ...), condition=%wide.region_5.6_spmd.clone.clone.clone, body=%wide.region_1.5_spmd.clone.clone.clone.sunk | while | flops 2536740608 | bytes 5860804 | solution.py:151
  626.6 12.8 fusion.144
  642.3 12.3 all-to-all-start.1
  659.8 66.1 %all-to-all-done.1 = bf16[8,512,384]{1,2,0:T(8,128)(2,1)S(1)} async-done(((bf16[8,512,384]{1,2,0:T(8,128)(2,1)}), bf16[8,512,384]{1,2,0:T(8,128)(2,1)S(1)}, u32[]{:S(2)}, u32[]{:S(2)}) %all-to-all-start.1) | async-done | bytes 3145760 | tf_op jit(solution)/shard_map/all_to_all | solution.py:236
  731.9 12.6 multiply_reduce_fusion.3
  756.1 70.7 %all-to-all-done.2 = bf16[512,8,384]{0,2,1:T(8,128)(2,1)S(1)} async-done(((bf16[512,8,384]{0,2,1:T(8,128)(2,1)}), bf16[512,8,384]{0,2,1:T(8,128)(2,1)S(1)}, u32[]{:S(2)}, u32[]{:S(2)}) %all-to-all-start.2) | async-done | bytes 3145760 | tf_op jit(solution)/shard_map/all_to_all | solution.py:255
  860.6 557.6 %while.74 = (s32[]{:T(128)}, f32[128,384]{1,0:T(8,128)S(1)}, f32[16,256,384]{2,1,0:T(8,128)}, f32[16,256,128]{2,1,0:T(8,128)}, f32[16,256,128]{2,1,0:T(8,128)}, ...) while((s32[]{:T(128)}, f32[128,384]{1,0:T(8,128)S(1)}, ...), condition=%wide.region_24.25_spmd.clone, body=%wide.region_14.24_spmd.clone.sunk | while | flops 5326403584 | bytes 15732097 | solution.py:151
  1445.8 11.0 pad_add_fusion.1
  1458.8 23.2 %multiply_reduce_fusion.6 = (f32[384]{0:T(512)}, f32[384]{0:T(512)}, f32[384]{0:T(512)}, bf16[384]{0:T(512)(128)(2,1)}, f32[384]{0:T(512)}, /*index=5*/f32[4096,...) fusion(f32[4096,384]{1,0:T(8,128)} %bitcast_convert_fusion, ...), kind=kLoop, calls=%fused_computation.197 | loop fusion | flops 51902208 | bytes 59832576 | tf_op jit(solution)/shard_map/transpose(jvp())/reduce_sum | solution.py:62
  1557.8 83.6 %reduce-scatter.15.cloned.1.call-done = bf16[512,304]{0,1:T(8,128)(2,1)} async-done(((bf16[4096,304]{0,1:T(8,128)(2,1)}), bf16[512,304]{0,1:T(8,128)(2,1)}) %reduce-scatter.15.cloned.1.call-update) | async-done | bytes 311312 | tf_op jit(solution)/shard_map/reduce_scatter | solution.py:287
  1641.4 17.4 convolution_convert_fusion
  1658.9 25.0 %copy.152 = bf16[1536,6448]{1,0:T(8,128)(2,1)} copy(bf16[1536,6448]{0,1:T(8,128)(2,1)} %convolution_convert_fusion) | data formatting | bytes 39616512
  1687.2 33.3 %reduce-scatter.19.cloned.1.call-done = bf16[768,1536]{1,0:T(8,128)(2,1)} async-done(((bf16[3072,1536]{1,0:T(8,128)(2,1)}), bf16[768,1536]{1,0:T(8,128)(2,1)}) %reduce-scatter.19.cloned.1.call-update) | async-done | bytes 2359312 | tf_op jit(solution)/shard_map/reduce_scatter | solution.py:332
  1720.5 149.7 %reduce-scatter.23.cloned.1.call-done = bf16[384,6448]{1,0:T(8,128)(2,1)} async-done(((bf16[1536,6448]{1,0:T(8,128)(2,1)}), bf16[384,6448]{1,0:T(8,128)(2,1)}) %reduce-scatter.23.cloned.1.call-update) | async-done | bytes 4952080
  1874.8 11.1 fusion.159
  1886.2 10.9 reduce-scatter.27.cloned.1.call-done
  1898.2 20.3 fusion.155
  1928.9 37.7 %all-reduce.33 = (bf16[384]{0:T(512)(128)(2,1)S(1)}, bf16[4,832]{1,0:T(4,128)(2,1)S(1)}, bf16[832]{0:T(1024)(128)(2,1)S(1)}, bf16[8,144]{1,0:T(8,128)(2,1)S(1)}, bf16[768]{0:T(1024)(128)(2,1)S(1)}) all-reduce(bf16[384]{0:T(512)(128)(2,1)S(1)} %dynamic-slice.41, ...), channel_id=6, replica_groups=mesh['shard'=4,'seq'=8] {'seq'}, use_global_device_ids=true, to_apply=%region_32.33.clone | all-reduce | flops 6464 | bytes 25856
  1974.7 17.7 reduce-scatter.21.cloned.1.call-done
  1994.2 100.6 %reduce-scatter.25.cloned.1.call-done = bf16[48,6448]{1,0:T(8,128)(2,1)} async-done(((bf16[384,6448]{1,0:T(8,128)(2,1)}), bf16[48,6448]{1,0:T(8,128)(2,1)}) %reduce-scatter.25.cloned.1.call-update) | async-done | bytes 619024
  (1532 shorter events, 1161.8 us)
Async XLA Ops:
  7.2 130.0 %all-gather.10.cloned.1.call-start = ((), (), s32[]{:S(2)}) async-start(), calls=%async_computation.11 | async-start | bytes 24760320 | tf_op jit(solution)/shard_map/all_gather | solution.py:180
  7.9 224.5 %all-gather.12.cloned.1.call-start = ((), (), s32[]{:S(2)}) async-start(), calls=%async_computation.12 | async-start | bytes 2801664 | tf_op jit(solution)/shard_map/all_gather | solution.py:203
  15.2 144.3 %copy-start.61 = (bf16[4,832]{1,0:T(4,128)(2,1)S(1)}, bf16[4,832]{1,0:T(4,128)(2,1)}, u32[]{:S(2)}) copy-start(bf16[4,832]{1,0:T(4,128)(2,1)} %param.35) | copy-start | bytes 19972
  15.2 149.6 %copy-start.71 = (u32[32]{0:T(128)S(1)}, u32[32]{0:T(128)}, u32[]{:S(2)}) copy-start(u32[32]{0:T(128)} %constant.423) | copy-start | bytes 388
  15.2 150.9 %copy-start.72 = (bf16[832]{0:T(1024)(128)(2,1)S(1)}, bf16[832]{0:T(1024)(128)(2,1)}, u32[]{:S(2)}) copy-start(bf16[832]{0:T(1024)(128)(2,1)} %param.36) | copy-start | bytes 4996
  15.2 160.0 %copy-start.86 = (bf16[48]{0:T(256)(128)(2,1)S(1)}, bf16[48]{0:T(256)(128)(2,1)}, u32[]{:S(2)}) copy-start(bf16[48]{0:T(256)(128)(2,1)} %param.39) | copy-start | bytes 292
  155.9 576.0 %all-gather.14.cloned.1.call-start = ((), (), s32[]{:S(2)}) async-start(), calls=%async_computation.13 | async-start | bytes 11796480 | tf_op jit(solution)/shard_map/all_gather | solution.py:184
  179.9 95.5 %all-to-all-start = ((bf16[512,8,384]{0,2,1:T(8,128)(2,1)}), bf16[512,8,384]{0,2,1:T(8,128)(2,1)S(1)}, u32[]{:S(2)}, u32[]{:S(2)}) async-start(bf16[512,8,384]{0,2,1:T(8,128)(2,1)} %bitcast.462), calls=%async_computation | async-start | bytes 6291456 | tf_op jit(solution)/shard_map/all_to_all | solution.py:202
  234.0 21.4 %collective-permute-start = (bf16[3,256]{0,1:T(8,128)(2,1)}, bf16[3,256]{0,1:T(8,128)(2,1)}, u32[]{:S(2)}, u32[]{:S(2)}) collective-permute-start(bf16[3,256]{0,1:T(8,128)(2,1)} %slice.392), channel_id=1, source_target_pairs={{0,8},{8,16},{16,24},{1,9},{9,17},{17,25},{2,10},{10,18},{18,26},{... | collective-permute-start | bytes 4616 | tf_op jit(solution)/shard_map/ppermute | solution.py:16
  280.7 5.3 collective-permute-start.1
  309.5 317.1 %copy-start.69 = (f32[384]{0:T(512)S(1)}, f32[384]{0:T(512)}, u32[]{:S(2)}) copy-start(f32[384]{0:T(512)} %convolution_reduce_fusion) | copy-start | bytes 4612
  642.3 83.7 %all-to-all-start.1 = ((bf16[8,512,384]{1,2,0:T(8,128)(2,1)}), bf16[8,512,384]{1,2,0:T(8,128)(2,1)S(1)}, u32[]{:S(2)}, u32[]{:S(2)}) async-start(bf16[8,512,384]{1,2,0:T(8,128)(2,1)} %copy.135), calls=%async_computation.1 | async-start | bytes 6291456 | tf_op jit(solution)/shard_map/all_to_all | solution.py:236
  752.2 74.6 %all-to-all-start.2 = ((bf16[512,8,384]{0,2,1:T(8,128)(2,1)}), bf16[512,8,384]{0,2,1:T(8,128)(2,1)S(1)}, u32[]{:S(2)}, u32[]{:S(2)}) async-start(bf16[512,8,384]{0,2,1:T(8,128)(2,1)} %bitcast.464), calls=%async_computation.2 | async-start | bytes 6291456 | tf_op jit(solution)/shard_map/all_to_all | solution.py:255
  755.9 885.5 %reduce-scatter.15.cloned.1.call-start = ((), (), s32[]{:S(2)}) async-start(), calls=%async_computation.14 | async-start | bytes 2801664 | tf_op jit(solution)/shard_map/reduce_scatter | solution.py:287
  1506.9 10.3 collective-permute-start.3
  1521.1 199.4 %reduce-scatter.19.cloned.1.call-start = ((), (), s32[]{:S(2)}) async-start(), calls=%async_computation.16 | async-start | bytes 11796480 | tf_op jit(solution)/shard_map/reduce_scatter | solution.py:332
  1538.0 9.2 collective-permute-start.2
  1553.2 88.3 %all-to-all-start.3 = ((bf16[8,512,384]{1,2,0:T(8,128)(2,1)}), bf16[8,512,384]{1,2,0:T(8,128)(2,1)}, u32[]{:S(2)}, u32[]{:S(2)}) async-start(bf16[8,512,384]{1,2,0:T(8,128)(2,1)} %copy.141), calls=%async_computation.3 | async-start | bytes 6291456 | tf_op jit(solution)/shard_map/all_to_all | solution.py:284
  1557.8 312.5 %reduce-scatter.23.cloned.1.call-start = ((), (), s32[]{:S(2)}) async-start(), calls=%async_computation.18 | async-start | bytes 25067520
  1684.0 213.1 %reduce-scatter.27.cloned.1.call-start = ((), (), s32[]{:S(2)}) async-start(), calls=%async_computation.20 | async-start | bytes 1064960
  1685.9 186.3 %copy-start.89 = (u32[32]{0:T(128)S(1)}, u32[32]{0:T(128)}, u32[]{:S(2)}) copy-start(u32[32]{0:T(128)} %constant.433) | copy-start | bytes 388
  1686.1 242.8 %reduce-scatter.17.cloned.1.call-start = ((), (), s32[]{:S(2)}) async-start(), calls=%async_computation.15 | async-start | bytes 20480 | tf_op jit(solution)/shard_map/reduce_scatter | solution.py:335
  1687.1 305.3 %reduce-scatter.21.cloned.1.call-start = ((), (), s32[]{:S(2)}) async-start(), calls=%async_computation.17 | async-start | bytes 2654208 | tf_op jit(solution)/shard_map/reduce_scatter | solution.py:355
  1720.5 374.4 %reduce-scatter.25.cloned.1.call-start = ((), (), s32[]{:S(2)}) async-start(), calls=%async_computation.19 | async-start | bytes 5640192
  (88 other events, 2087.5 us)
Sparse Core Ops, SparseCore 0:
  9.6 127.5 all-gather.9
  156.0 76.4 all-gather.11
  234.0 75.5 all-gather.13
  1521.2 120.1 reduce-scatter.14
  1644.0 76.3 reduce-scatter.18
  1723.1 147.1 reduce-scatter.22
  1873.4 23.6 reduce-scatter.26
  1900.2 19.3 reduce-scatter.16
  1923.1 69.2 reduce-scatter.20
  1995.9 98.9 reduce-scatter.24
where the time goes:
time: 2120 us; the launch traced here: 2110 us
  waiting for transfers between devices  708 us (33%)
  matrix products  579 us (27%)
  other arithmetic  393 us (19%)
  local copies, waits for them, and re-layouts  278 us (13%)
  blocking collectives  89 us (4%)
  starting transfers between devices  33.7 us (2%)
    unnamed x13, waiting for transfers between devices  263 us
    another operation x102, other arithmetic  231 us
    dot_general x48, matrix products, block_step(): jnp.einsum('jts,sc->jtc', weights * scores[None], x_block, precision=HIGH)  198 us
    all_gather x1, waiting for transfers between devices, on_device(): lax.all_gather(in_weight, 'shard', axis=0, tiled=True)  122 us
    reduce_scatter x1, waiting for transfers between devices, on_device(): lax.psum_scatter(jnp.concatenate([d_bc_raw, d_dt_raw], 1).astype(jnp.bflo...  83.6 us
    all_to_all x1, waiting for transfers between devices, on_device(): lax.all_to_all(d_mixer.astype(jnp.bfloat16), 'seq', split_axis=1, concat_...  70.7 us
    all_to_all x1, waiting for transfers between devices, on_device(): lax.all_to_all(mixer_full.astype(jnp.bfloat16), 'seq', split_axis=0, conc...  66.1 us
    dot_general x64, matrix products, block_step(): scores = jnp.dot(c_block, b_block.T, precision=HIGH)  64.3 us
  transfers between devices with their start and end apart: 18, of which 11 were waited for; matrix products, arithmetic and copies ran while one was open for 25% of the time, Pallas kernels for 0%

commit v1 on v0

--- a/solution.py
+++ b/solution.py
@@ -8,6 +8,18 @@
 BLOCK = 256
 HIGH = lax.Precision.HIGHEST
 EPS = 1e-05
+
+
+def doubled_up(array, axis, dim):
+    ways, here, step = (lax.axis_size(axis), lax.axis_index(axis), array.shape[dim])
+    line, have = (array, 1)
+    while have < ways:
+        line = jnp.concatenate(
+            [line, lax.ppermute(line, axis, [(d, (d - have) % ways) for d in range(ways)])],
+            axis=dim,
+        )
+        have = 2 * have
+    return jnp.roll(line, here * step, axis=dim)
 
 
 def from_behind(value, axis, steps):
@@ -177,7 +189,7 @@
 ):
     gains_in, w_in, w_conv, b_conv, gains_out, w_out = (
         lax.all_gather(norm_gain, "shard", axis=0, tiled=True),
-        lax.all_gather(in_weight, "shard", axis=0, tiled=True),
+        doubled_up(in_weight, "shard", 0),
         lax.all_gather(conv_weight, "shard", axis=1, tiled=True),
         lax.all_gather(conv_bias, "shard", axis=0, tiled=True),
         lax.all_gather(out_gain, "shard", axis=0, tiled=True),

time: 2120 us -> 2310 us (1.090)
  blocking collectives: 89 us -> 300 us
  waiting for transfers between devices: 708 us -> 637 us
  local copies, waits for them, and re-layouts: 278 us -> 312 us
    all_gather x1, blocking collectives: 6.09 us -> 216 us  [on_device(): lax.all_gather(norm_gain, 'shard', axis=0, tiled=True)]
    all_gather x1 -> x0, waiting for transfers between devices: 122 us -> none  [on_device(): lax.all_gather(in_weight, 'shard', axis=0, tiled=True)]
    ppermute x0 -> x2, waiting for transfers between devices: none -> 54.5 us  [doubled_up(): lax.ppermute(line, axis, [(d, (d - have) % ways) for d in range(ways)])]
    unnamed x209 -> x216, local copies, waits for them, and re-layouts: 51.5 us -> 76.9 us
    unnamed x13 -> x12, waiting for transfers between devices: 263 us -> 262 us
  transfers between devices with their start and end apart: 18 -> 19, of which waited for: 11 -> 11; matrix products, arithmetic and copies ran while one was open for 25% -> 23% of each run, Pallas kernels for 0% -> 0%
where the time goes in v1:
time: 2310 us; the launch traced here: 2300 us
  waiting for transfers between devices  637 us (28%)
  matrix products  582 us (25%)
  other arithmetic  404 us (17%)
  local copies, waits for them, and re-layouts  312 us (14%)
  blocking collectives  300 us (13%)
  starting transfers between devices  37.3 us (2%)
    unnamed x12, waiting for transfers between devices  262 us
    another operation x102, other arithmetic  232 us
    all_gather x1, blocking collectives, on_device(): lax.all_gather(norm_gain, 'shard', axis=0, tiled=True)  216 us
    dot_general x48, matrix products, block_step(): jnp.einsum('jts,sc->jtc', weights * scores[None], x_block, precision=HIGH)  198 us
    reduce_scatter x1, waiting for transfers between devices, on_device(): lax.psum_scatter(jnp.concatenate([d_bc_raw, d_dt_raw], 1).astype(jnp.bflo...  83.6 us
    unnamed x216, local copies, waits for them, and re-layouts  76.9 us
    all_to_all x1, waiting for transfers between devices, on_device(): lax.all_to_all(d_mixer.astype(jnp.bfloat16), 'seq', split_axis=1, concat_...  70.4 us
    all_to_all x1, waiting for transfers between devices, on_device(): lax.all_to_all(mixer_full.astype(jnp.bfloat16), 'seq', split_axis=0, conc...  66.1 us
  transfers between devices with their start and end apart: 19, of which 11 were waited for; matrix products, arithmetic and copies ran while one was open for 23% of the time, Pallas kernels for 0%

profile of v1, /device:TPU:0, one launch (start us, length us, event | category | flops | bytes accessed | tf_op | source)
XLA Modules:
  0.0 2296.5 jit_solution(7349704793918331494)
XLA Ops:
  9.7 54.5 %collective-permute-done = bf16[384,6448]{0,1:T(8,128)(2,1)S(1)} collective-permute-done((bf16[384,6448]{0,1:T(8,128)(2,1)}, bf16[384,6448]{0,1:T(8,128)(2,1)S(1)}, u32[]{:S(2)}, u32[]{:S(2)}) %collective-permute-start) | collective-permute-done | bytes 4952096 | tf_op jit(solution)/shard_map/ppermute | solution.py:18
  72.4 216.2 %all-gather.2 = bf16[4,1,384]{2,1,0:T(2,128)(2,1)S(1)} all-gather(bf16[1,1,384]{2,1,0:T(2,128)(2,1)S(1)} %reshape.682), channel_id=1, replica_groups=mesh['shard'=4,'seq'=8] {'shard'}, dimensions={0}, use_global_device_ids=true | all-gather | bytes 3840 | tf_op jit(solution)/shard_map/all_gather | solution.py:191
  324.8 17.6 fusion.135
  374.2 47.1 %all-gather.9.cloned.1.call-done = bf16[4096,304]{0,1:T(8,128)(2,1)} async-done(((bf16[512,304]{0,1:T(8,128)(2,1)}), bf16[4096,304]{0,1:T(8,128)(2,1)}) %all-gather.9.cloned.1.call-update) | async-done | bytes 2490384 | tf_op jit(solution)/shard_map/all_gather | solution.py:215
  474.8 19.7 fusion.206
  497.8 309.6 %while.75 = (s32[]{:T(128)}, f32[128,384]{1,0:T(8,128)S(1)}, f32[16,256,384]{2,1,0:T(8,128)}, f32[16,128,384]{2,1,0:T(8,128)}, f32[16,256,7]{1,2,0:T(8,128)}, /*...) while((s32[]{:T(128)}, f32[128,384]{1,0:T(8,128)S(1)}, ...), condition=%wide.region_5.6_spmd.clone.clone.clone, body=%wide.region_1.5_spmd.clone.clone.clone.sunk | while | flops 2536740608 | bytes 5860804 | solution.py:163
  814.6 12.8 fusion.151
  830.3 12.9 all-to-all-start.1
  848.4 66.1 %all-to-all-done.1 = bf16[8,512,384]{1,2,0:T(8,128)(2,1)S(1)} async-done(((bf16[8,512,384]{1,2,0:T(8,128)(2,1)}), bf16[8,512,384]{1,2,0:T(8,128)(2,1)S(1)}, u32[]{:S(2)}, u32[]{:S(2)}) %all-to-all-start.1) | async-done | bytes 3145760 | tf_op jit(solution)/shard_map/all_to_all | solution.py:248
  920.4 12.6 multiply_reduce_fusion.3
  944.9 70.4 %all-to-all-done.2 = bf16[512,8,384]{0,2,1:T(8,128)(2,1)S(1)} async-done(((bf16[512,8,384]{0,2,1:T(8,128)(2,1)}), bf16[512,8,384]{0,2,1:T(8,128)(2,1)S(1)}, u32[]{:S(2)}, u32[]{:S(2)}) %all-to-all-start.2) | async-done | bytes 3145760 | tf_op jit(solution)/shard_map/all_to_all | solution.py:267
  1049.2 557.3 %while.74 = (s32[]{:T(128)}, f32[128,384]{1,0:T(8,128)S(1)}, f32[16,256,384]{2,1,0:T(8,128)}, f32[16,256,128]{2,1,0:T(8,128)}, f32[16,256,128]{2,1,0:T(8,128)}, ...) while((s32[]{:T(128)}, f32[128,384]{1,0:T(8,128)S(1)}, ...), condition=%wide.region_24.25_spmd.clone, body=%wide.region_14.24_spmd.clone.sunk | while | flops 5326403584 | bytes 15732097 | solution.py:163
  1636.4 11.0 pad_add_fusion.1
  1649.5 23.3 %multiply_reduce_fusion.6 = (f32[384]{0:T(512)}, f32[384]{0:T(512)}, f32[384]{0:T(512)}, bf16[384]{0:T(512)(128)(2,1)}, f32[384]{0:T(512)}, /*index=5*/f32[4096,...) fusion(f32[4096,384]{1,0:T(8,128)} %bitcast_convert_fusion, ...), kind=kLoop, calls=%fused_computation.202 | loop fusion | flops 51902208 | bytes 59832576 | tf_op jit(solution)/shard_map/transpose(jvp())/reduce_sum | solution.py:74
  1748.4 83.6 %reduce-scatter.15.cloned.1.call-done = bf16[512,304]{0,1:T(8,128)(2,1)} async-done(((bf16[4096,304]{0,1:T(8,128)(2,1)}), bf16[512,304]{0,1:T(8,128)(2,1)}) %reduce-scatter.15.cloned.1.call-update) | async-done | bytes 311312 | tf_op jit(solution)/shard_map/reduce_scatter | solution.py:299
  1832.0 17.3 convolution_convert_fusion
  1849.3 25.4 %copy.152 = bf16[1536,6448]{1,0:T(8,128)(2,1)} copy(bf16[1536,6448]{0,1:T(8,128)(2,1)} %convolution_convert_fusion) | data formatting | bytes 39616512
  1878.0 33.0 %reduce-scatter.19.cloned.1.call-done = bf16[768,1536]{1,0:T(8,128)(2,1)} async-done(((bf16[3072,1536]{1,0:T(8,128)(2,1)}), bf16[768,1536]{1,0:T(8,128)(2,1)}) %reduce-scatter.19.cloned.1.call-update) | async-done | bytes 2359312 | tf_op jit(solution)/shard_map/reduce_scatter | solution.py:344
  1911.1 149.7 %reduce-scatter.23.cloned.1.call-done = bf16[384,6448]{1,0:T(8,128)(2,1)} async-done(((bf16[1536,6448]{1,0:T(8,128)(2,1)}), bf16[384,6448]{1,0:T(8,128)(2,1)}) %reduce-scatter.23.cloned.1.call-update) | async-done | bytes 4952080
  2065.3 11.3 fusion.166
  2088.6 21.3 fusion.162
  2120.4 37.8 %all-reduce.33 = (bf16[384]{0:T(512)(128)(2,1)S(1)}, bf16[4,832]{1,0:T(4,128)(2,1)S(1)}, bf16[832]{0:T(1024)(128)(2,1)S(1)}, bf16[8,144]{1,0:T(8,128)(2,1)S(1)}, bf16[768]{0:T(1024)(128)(2,1)S(1)}) all-reduce(bf16[384]{0:T(512)(128)(2,1)S(1)} %dynamic-slice.41, ...), channel_id=6, replica_groups=mesh['shard'=4,'seq'=8] {'seq'}, use_global_device_ids=true, to_apply=%region_32.33.clone | all-reduce | flops 6464 | bytes 25856
  2166.2 16.6 reduce-scatter.21.cloned.1.call-done
  2184.7 100.8 %reduce-scatter.25.cloned.1.call-done = bf16[48,6448]{1,0:T(8,128)(2,1)} async-done(((bf16[384,6448]{1,0:T(8,128)(2,1)}), bf16[48,6448]{1,0:T(8,128)(2,1)}) %reduce-scatter.25.cloned.1.call-update) | async-done | bytes 619024
  (1542 shorter events, 1212.1 us)
Async XLA Ops:
  7.2 281.4 %copy-start.22 = (bf16[512,1536]{1,0:T(8,128)(2,1)S(1)}, bf16[512,1536]{1,0:T(8,128)(2,1)}, u32[]{:S(2)}) copy-start(bf16[512,1536]{1,0:T(8,128)(2,1)} %param.30) | copy-start | bytes 4718596
  7.2 414.1 %all-gather.9.cloned.1.call-start = ((), (), s32[]{:S(2)}) async-start(), calls=%async_computation.11 | async-start | bytes 2801664 | tf_op jit(solution)/shard_map/all_gather | solution.py:215
  7.2 56.9 %collective-permute-start = (bf16[384,6448]{0,1:T(8,128)(2,1)}, bf16[384,6448]{0,1:T(8,128)(2,1)S(1)}, u32[]{:S(2)}, u32[]{:S(2)}) collective-permute-start(bf16[384,6448]{0,1:T(8,128)(2,1)} %param.34), channel_id=1, source_target_pairs={{0,24},{8,0},{16,8},{24,16},{1,25},{9,1},{17,9},{25,17},{2,26},{10... | collective-permute-start | bytes 14856200 | tf_op jit(solution)/shard_map/ppermute | solution.py:18
  71.8 225.6 %collective-permute-start.1 = (bf16[768,6448]{0,1:T(8,128)(2,1)}, bf16[768,6448]{0,1:T(8,128)(2,1)}, u32[]{:S(2)}, u32[]{:S(2)}) collective-permute-start(bf16[768,6448]{0,1:T(8,128)(2,1)} %pad_maximum_fusion), channel_id=1, source_target_pairs={{0,16},{8,24},{16,0},{24,8},{1,17},{9,25},{17,1},{25,9},{2,18},{10... | collective-permute-start | bytes 29712392 | tf_op jit(solution)/shard_map/ppermute | solution.py:18
  344.1 576.3 %all-gather.11.cloned.1.call-start = ((), (), s32[]{:S(2)}) async-start(), calls=%async_computation.12 | async-start | bytes 11796480 | tf_op jit(solution)/shard_map/all_gather | solution.py:196
  368.7 95.6 %all-to-all-start = ((bf16[512,8,384]{0,2,1:T(8,128)(2,1)}), bf16[512,8,384]{0,2,1:T(8,128)(2,1)S(1)}, u32[]{:S(2)}, u32[]{:S(2)}) async-start(bf16[512,8,384]{0,2,1:T(8,128)(2,1)} %bitcast.460), calls=%async_computation | async-start | bytes 6291456 | tf_op jit(solution)/shard_map/all_to_all | solution.py:214
  422.9 21.2 collective-permute-start.2
  469.5 5.2 collective-permute-start.3
  497.8 316.8 %copy-start.70 = (f32[384]{0:T(512)S(1)}, f32[384]{0:T(512)}, u32[]{:S(2)}) copy-start(f32[384]{0:T(512)} %convolution_reduce_fusion) | copy-start | bytes 4612
  830.3 84.3 %all-to-all-start.1 = ((bf16[8,512,384]{1,2,0:T(8,128)(2,1)}), bf16[8,512,384]{1,2,0:T(8,128)(2,1)S(1)}, u32[]{:S(2)}, u32[]{:S(2)}) async-start(bf16[8,512,384]{1,2,0:T(8,128)(2,1)} %copy.135), calls=%async_computation.1 | async-start | bytes 6291456 | tf_op jit(solution)/shard_map/all_to_all | solution.py:248
  940.8 74.6 %all-to-all-start.2 = ((bf16[512,8,384]{0,2,1:T(8,128)(2,1)}), bf16[512,8,384]{0,2,1:T(8,128)(2,1)S(1)}, u32[]{:S(2)}, u32[]{:S(2)}) async-start(bf16[512,8,384]{0,2,1:T(8,128)(2,1)} %bitcast.462), calls=%async_computation.2 | async-start | bytes 6291456 | tf_op jit(solution)/shard_map/all_to_all | solution.py:267
  944.5 887.4 %reduce-scatter.15.cloned.1.call-start = ((), (), s32[]{:S(2)}) async-start(), calls=%async_computation.13 | async-start | bytes 2801664 | tf_op jit(solution)/shard_map/reduce_scatter | solution.py:299
  1697.5 10.2 collective-permute-start.5
  1711.7 199.4 %reduce-scatter.19.cloned.1.call-start = ((), (), s32[]{:S(2)}) async-start(), calls=%async_computation.15 | async-start | bytes 11796480 | tf_op jit(solution)/shard_map/reduce_scatter | solution.py:344
  1728.5 9.2 collective-permute-start.4
  1739.1 92.9 %copy-start.34 = (f32[1536]{0:T(1024)S(1)}, f32[1536]{0:T(1024)}, u32[]{:S(2)}) copy-start(f32[1536]{0:T(1024)} %copy-done.33) | copy-start | bytes 18436
  1739.1 92.9 %copy-start.58 = (f32[512]{0:T(512)S(1)}, f32[512]{0:T(512)}, u32[]{:S(2)}) copy-start(f32[512]{0:T(512)} %copy-done.57) | copy-start | bytes 6148
  1743.9 88.1 %all-to-all-start.3 = ((bf16[8,512,384]{1,2,0:T(8,128)(2,1)}), bf16[8,512,384]{1,2,0:T(8,128)(2,1)}, u32[]{:S(2)}, u32[]{:S(2)}) async-start(bf16[8,512,384]{1,2,0:T(8,128)(2,1)} %copy.141), calls=%async_computation.3 | async-start | bytes 6291456 | tf_op jit(solution)/shard_map/all_to_all | solution.py:296
  1748.3 312.5 %reduce-scatter.23.cloned.1.call-start = ((), (), s32[]{:S(2)}) async-start(), calls=%async_computation.17 | async-start | bytes 25067520
  1874.8 188.0 %copy-start.90 = (u32[32]{0:T(128)S(1)}, u32[32]{0:T(128)}, u32[]{:S(2)}) copy-start(u32[32]{0:T(128)} %constant.451) | copy-start | bytes 388
  1874.8 212.7 %reduce-scatter.27.cloned.1.call-start = ((), (), s32[]{:S(2)}) async-start(), calls=%async_computation.19 | async-start | bytes 1064960
  1876.9 243.4 %reduce-scatter.17.cloned.1.call-start = ((), (), s32[]{:S(2)}) async-start(), calls=%async_computation.14 | async-start | bytes 20480 | tf_op jit(solution)/shard_map/reduce_scatter | solution.py:347
  1878.0 304.9 %reduce-scatter.21.cloned.1.call-start = ((), (), s32[]{:S(2)}) async-start(), calls=%async_computation.16 | async-start | bytes 2654208 | tf_op jit(solution)/shard_map/reduce_scatter | solution.py:367
  1911.0 374.4 %reduce-scatter.25.cloned.1.call-start = ((), (), s32[]{:S(2)}) async-start(), calls=%async_computation.18 | async-start | bytes 5640192
  (90 other events, 1593.4 us)
Sparse Core Ops, SparseCore 0:
  344.3 76.9 all-gather.8
  422.8 75.6 all-gather.10
  1711.8 120.1 reduce-scatter.14
  1834.6 76.3 reduce-scatter.18
  1913.6 147.1 reduce-scatter.22
  2063.8 23.6 reduce-scatter.26
  2090.6 19.2 reduce-scatter.16
  2113.4 69.3 reduce-scatter.20
  2186.5 98.9 reduce-scatter.24
